TPU v7x, 32 devices: a whole 2x2x4 slice. The times are simulated.
32 devices in a mesh: row: 8 (over z, y), col: 4 (over x, core).
Axes of the slice: x: 2, y: 2, z: 4, core: 2. Of those that a mesh axis runs over, the one named last changes fastest.
Arguments:
- tokens_in: bfloat16 [10240, 1024], P('row', 'col'), may hold values from -6 to 6
- grad_out: bfloat16 [10240, 1024], P('row', 'col'), may hold values from -6 to 6
- keep_mask: int32 [32, 256], P('row'), may hold values 0 or 1
- adapter_index: int32 [32], P('row'), may hold values from 0 to 7
- ln_gain: float32 [2, 1024], replicated, may hold values from 0.25 to 1.75
- ln_shift: float32 [2, 1024], replicated, may hold values from -1.8 to 1.8
- w_qkv: bfloat16 [3, 1024, 1024], P(None, 'row', 'col'), may hold values from -0.1875 to 0.1875
- bias_qv: bfloat16 [2, 1024], P(None, 'col'), may hold values from -1.796875 to 1.796875
- w_proj: bfloat16 [1024, 1024], P('col', 'row'), may hold values from -1.5 to 1.5
- w_fc1: bfloat16 [1024, 4096], P('row', 'col'), may hold values from -0.1875 to 0.1875
- bias_fc1: bfloat16 [4096], P('col'), may hold values from -1.796875 to 1.796875
- w_fc2: bfloat16 [4096, 1024], P('col', 'row'), may hold values from -0.09375 to 0.09375
- bias_out: bfloat16 [2, 1024], replicated, may hold values from -1.796875 to 1.796875
- qkv_down: bfloat16 [8, 16, 1024], replicated, may hold values from -0.1875 to 0.1875
- qkv_up: bfloat16 [8, 16, 3, 1024], replicated, may hold values from -0.75 to 0.75
- proj_down: bfloat16 [8, 16, 1024], replicated, may hold values from -1.5 to 1.5
- proj_up: bfloat16 [8, 16, 1024], replicated, may hold values from -0.75 to 0.75
- fc1_down: bfloat16 [8, 16, 1024], replicated, may hold values from -0.1875 to 0.1875
- fc1_up: bfloat16 [8, 16, 4096], replicated, may hold values from -0.75 to 0.75
- fc2_down: bfloat16 [8, 16, 4096], replicated, may hold values from -0.09375 to 0.09375
- fc2_up: bfloat16 [8, 16, 1024], replicated, may hold values from -0.75 to 0.75
Outputs:
- layer_out: bfloat16 [10240, 1024], P('row', 'col')
- grad_in: bfloat16 [10240, 1024], P('row', 'col')
- grad_qkv_down: float32 [8, 16, 1024], replicated
- grad_qkv_up: float32 [8, 16, 3, 1024], replicated
- grad_proj_down: float32 [8, 16, 1024], replicated
- grad_proj_up: float32 [8, 16, 1024], replicated
- grad_fc1_down: float32 [8, 16, 1024], replicated
- grad_fc1_up: float32 [8, 16, 4096], replicated
- grad_fc2_down: float32 [8, 16, 4096], replicated
- grad_fc2_up: float32 [8, 16, 1024], replicated
All inputs are finite; a program needn't handle non-finite values. No bound on the sum of `keep_mask` on one device may be relied on, other than what follows from the above.
Results may differ from a plain program's by a relative error of at most 0.013.
Values may be sent and summed in bfloat16 or wider, within the bound.
No kernel may reach another device: no remote copies, remote signals or barrier semaphores. Data moves between devices by JAX's collectives and lax.ppermute only.
A program may use at most 192 MiB of HBM per device.

v0:
```python
import jax
import jax.numpy as jnp
from jax import lax
from jax.sharding import PartitionSpec as P

D = 1024
H = 16
HD = 64
FF = 4096
BUF = 64
R = 16
NA = 8
SEQ = 320
highest = lax.Precision.HIGHEST


def norm_parts(values):
    row_mean = jnp.mean(values, axis=-1, keepdims=True)
    centered = values - row_mean
    variance = jnp.mean(centered * centered, axis=-1, keepdims=True)
    inverse = lax.rsqrt(variance + 1e-06)
    return (centered * inverse, inverse)


def norm_back(grad_normed, gain_row, unit_rows, inverse):
    scaled = grad_normed * gain_row
    first_mean = jnp.mean(scaled, axis=-1, keepdims=True)
    second_mean = jnp.mean(scaled * unit_rows, axis=-1, keepdims=True)
    return inverse * (scaled - first_mean - unit_rows * second_mean)


def gelu_slope(pre_gelu):
    cumulative = 0.5 * (1.0 + lax.erf(pre_gelu * 0.7071067811865476))
    return cumulative + pre_gelu * jnp.exp(-0.5 * pre_gelu * pre_gelu) * 0.3989422804014327


def narrow_dot(formula, left_side, right_side):
    return jnp.einsum(formula, left_side, right_side, preferred_element_type=jnp.float32)


def exact_dot(formula, left_side, right_side):
    return jnp.einsum(
        formula, left_side, right_side, precision=highest, preferred_element_type=jnp.float32
    )


def attention_pair(query_heads, key_heads, value_heads, key_open):

    def scores_of():
        raw_scores = narrow_dot("gqhd,gkhd->ghqk", query_heads, key_heads) * 0.125
        return jnp.where(key_open[:, None, None, :], raw_scores, -1e30)

    scores = scores_of()
    top_score = jnp.max(scores, axis=-1, keepdims=True)
    exponent = jnp.exp(scores - top_score)
    row_total = jnp.sum(exponent, axis=-1, keepdims=True)
    log_total = top_score + jnp.log(row_total)
    soft_low = (exponent / row_total).astype(jnp.bfloat16)
    attended = narrow_dot("ghqk,gkhd->gqhd", soft_low, value_heads)

    def backward(grad_heads):
        soft_again = jnp.exp(scores_of() - log_total)
        grad_values = narrow_dot("ghqk,gqhd->gkhd", soft_again.astype(jnp.bfloat16), grad_heads)
        grad_soft = narrow_dot("gqhd,gkhd->ghqk", grad_heads, value_heads)
        grad_scores = (
            soft_again * (grad_soft - jnp.sum(grad_soft * soft_again, axis=-1, keepdims=True))
        ).astype(jnp.bfloat16)
        grad_queries = narrow_dot("ghqk,gkhd->gqhd", grad_scores, key_heads) * 0.125
        grad_keys = narrow_dot("ghqk,gqhd->gkhd", grad_scores, query_heads) * 0.125
        return (grad_queries, grad_keys, grad_values)

    return (attended, backward)


def images_layer(
    x_rows,
    g_rows,
    keep_rows,
    select,
    key_open,
    ln_gain,
    ln_shift,
    w_qkv,
    bias_qv,
    w_proj,
    w_fc1,
    bias_fc1,
    w_fc2,
    bias_out,
    flats,
):
    (
        qkv_down_flat,
        qkv_up_flat,
        proj_down_flat,
        proj_up_flat,
        fc1_down_flat,
        fc1_up_flat,
        fc2_down_flat,
        fc2_up_flat,
    ) = flats
    images = key_open.shape[0]
    tok_rows = images * SEQ
    bias_pair = bias_qv.astype(jnp.float32)
    bias_pair_out = bias_out.astype(jnp.float32)
    hidden = x_rows.astype(jnp.float32)
    unit_one, inverse_one = norm_parts(hidden)
    normed_one = (unit_one * ln_gain[0] + ln_shift[0]).astype(jnp.bfloat16)
    latent_one = narrow_dot("td,rd->tr", normed_one, qkv_down_flat) * select
    projected = narrow_dot("td,cde->cte", normed_one, w_qkv) + exact_dot(
        "tr,rce->cte", latent_one, qkv_up_flat.astype(jnp.float32)
    )
    queries = (projected[0] + bias_pair[0]).astype(jnp.bfloat16)
    key_side = projected[1].astype(jnp.bfloat16)
    value_side = (projected[2] + bias_pair[1]).astype(jnp.bfloat16)
    head_shape = (images, SEQ, H, HD)
    attended_heads, attention_back = attention_pair(
        queries.reshape(head_shape),
        key_side.reshape(head_shape),
        value_side.reshape(head_shape),
        key_open,
    )
    attended = attended_heads.reshape(tok_rows, D).astype(jnp.bfloat16)
    latent_two = narrow_dot("th,rh->tr", attended, proj_down_flat) * select
    branch = (
        narrow_dot("th,hd->td", attended, w_proj)
        + exact_dot("tr,rd->td", latent_two, proj_up_flat.astype(jnp.float32))
        + bias_pair_out[0]
    )
    middle = hidden + branch
    unit_two, inverse_two = norm_parts(middle)
    normed_two = (unit_two * ln_gain[1] + ln_shift[1]).astype(jnp.bfloat16)
    latent_three = narrow_dot("td,rd->tr", normed_two, fc1_down_flat) * select
    pre_gelu = (
        narrow_dot("td,df->tf", normed_two, w_fc1)
        + exact_dot("tr,rf->tf", latent_three, fc1_up_flat.astype(jnp.float32))
        + bias_fc1.astype(jnp.float32)
    )
    activated = jax.nn.gelu(pre_gelu, approximate=False).astype(jnp.bfloat16)
    latent_four = narrow_dot("tf,rf->tr", activated, fc2_down_flat) * select
    result = (
        narrow_dot("tf,fd->td", activated, w_fc2)
        + exact_dot("tr,rd->td", latent_four, fc2_up_flat.astype(jnp.float32))
        + bias_pair_out[1]
    )
    out_rows = (keep_rows * (middle + result)).astype(jnp.bfloat16)
    grad_result = g_rows.astype(jnp.float32) * keep_rows
    grad_result_low = grad_result.astype(jnp.bfloat16)
    grad_latent_four = narrow_dot("td,rd->tr", grad_result_low, fc2_up_flat) * select
    grad_act = narrow_dot("td,fd->tf", grad_result_low, w_fc2) + exact_dot(
        "tr,rf->tf", grad_latent_four, fc2_down_flat.astype(jnp.float32)
    )
    grad_pre = (grad_act * gelu_slope(pre_gelu)).astype(jnp.bfloat16)
    grad_latent_three = narrow_dot("tf,rf->tr", grad_pre, fc1_up_flat) * select
    grad_normed_two = narrow_dot("tf,df->td", grad_pre, w_fc1) + exact_dot(
        "tr,rd->td", grad_latent_three, fc1_down_flat.astype(jnp.float32)
    )
    grad_fc2_up = exact_dot("tr,td->rd", latent_four, grad_result)
    grad_fc2_down = exact_dot("tr,tf->rf", grad_latent_four, activated.astype(jnp.float32))
    grad_fc1_up = exact_dot("tr,tf->rf", latent_three, grad_pre.astype(jnp.float32))
    grad_fc1_down = exact_dot("tr,td->rd", grad_latent_three, normed_two.astype(jnp.float32))
    grad_middle = grad_result + norm_back(grad_normed_two, ln_gain[1], unit_two, inverse_two)
    grad_branch = grad_middle.astype(jnp.bfloat16)
    grad_latent_two = narrow_dot("td,rd->tr", grad_branch, proj_up_flat) * select
    grad_attended = (
        narrow_dot("td,hd->th", grad_branch, w_proj)
        + exact_dot("tr,rh->th", grad_latent_two, proj_down_flat.astype(jnp.float32))
    ).astype(jnp.bfloat16)
    grad_proj_up = exact_dot("tr,td->rd", latent_two, grad_branch.astype(jnp.float32))
    grad_proj_down = exact_dot("tr,th->rh", grad_latent_two, attended.astype(jnp.float32))
    grad_queries, grad_keys, grad_values = attention_back(grad_attended.reshape(head_shape))
    grad_qkv = (
        jnp.stack([grad_queries, grad_keys, grad_values])
        .reshape(3, tok_rows, D)
        .astype(jnp.bfloat16)
    )
    grad_latent_one = narrow_dot("cte,rce->tr", grad_qkv, qkv_up_flat) * select
    grad_normed_one = narrow_dot("cte,cde->td", grad_qkv, w_qkv) + exact_dot(
        "tr,rd->td", grad_latent_one, qkv_down_flat.astype(jnp.float32)
    )
    grad_qkv_up = exact_dot("tr,cte->rce", latent_one, grad_qkv.astype(jnp.float32))
    grad_qkv_down = exact_dot("tr,td->rd", grad_latent_one, normed_one.astype(jnp.float32))
    grad_hidden = grad_middle + norm_back(grad_normed_one, ln_gain[0], unit_one, inverse_one)
    grads = (
        grad_qkv_down,
        grad_qkv_up,
        grad_proj_down,
        grad_proj_up,
        grad_fc1_down,
        grad_fc1_up,
        grad_fc2_down,
        grad_fc2_up,
    )
    return (out_rows, grad_hidden.astype(jnp.bfloat16), grads)


def per_device(
    tokens_in,
    grad_out,
    keep_mask,
    adapter_index,
    ln_gain,
    ln_shift,
    w_qkv,
    bias_qv,
    w_proj,
    w_fc1,
    bias_fc1,
    w_fc2,
    bias_out,
    qkv_down,
    qkv_up,
    proj_down,
    proj_up,
    fc1_down,
    fc1_up,
    fc2_down,
    fc2_up,
):
    columns = lax.axis_size("col")
    column = lax.axis_index("col")
    images = adapter_index.shape[0]
    tok_rows = images * SEQ
    rank_total = NA * R
    keep_full = jnp.concatenate([jnp.ones((images, BUF), jnp.int32), keep_mask], axis=1)
    key_open = keep_full > 0
    keep_rows = keep_full.reshape(tok_rows, 1).astype(jnp.float32)
    owner_rows = jnp.broadcast_to(adapter_index[:, None], (images, SEQ)).reshape(tok_rows, 1)
    select = (owner_rows == lax.broadcasted_iota(jnp.int32, (1, rank_total), 1) // R).astype(
        jnp.float32
    )
    flats = (
        qkv_down.reshape(rank_total, D),
        qkv_up.reshape(rank_total, 3, D),
        proj_down.reshape(rank_total, D),
        proj_up.reshape(rank_total, D),
        fc1_down.reshape(rank_total, D),
        fc1_up.reshape(rank_total, FF),
        fc2_down.reshape(rank_total, FF),
        fc2_up.reshape(rank_total, D),
    )
    qkv_cols, proj_rows, fc1_cols, fc2_rows = (
        lax.all_gather(w_qkv, "row", axis=1, tiled=True),
        lax.all_gather(w_proj, "row", axis=1, tiled=True),
        lax.all_gather(w_fc1, "row", axis=0, tiled=True),
        lax.all_gather(w_fc2, "row", axis=1, tiled=True),
    )
    qkv_full, proj_full, fc1_full, fc2_full, bias_qv_full, bias_fc1_full = (
        lax.all_gather(qkv_cols, "col", axis=2, tiled=True),
        lax.all_gather(proj_rows, "col", axis=0, tiled=True),
        lax.all_gather(fc1_cols, "col", axis=1, tiled=True),
        lax.all_gather(fc2_rows, "col", axis=0, tiled=True),
        lax.all_gather(bias_qv, "col", axis=1, tiled=True),
        lax.all_gather(bias_fc1, "col", axis=0, tiled=True),
    )
    x_rows, g_rows = (
        lax.all_to_all(tokens_in, "col", split_axis=0, concat_axis=1, tiled=True),
        lax.all_to_all(grad_out, "col", split_axis=0, concat_axis=1, tiled=True),
    )
    local_images = images // columns
    slice_rows = local_images * SEQ
    row_start = column * slice_rows
    out_rows, grad_rows, grads = images_layer(
        x_rows,
        g_rows,
        lax.dynamic_slice_in_dim(keep_rows, row_start, slice_rows, 0),
        lax.dynamic_slice_in_dim(select, row_start, slice_rows, 0),
        lax.dynamic_slice_in_dim(key_open, column * local_images, local_images, 0),
        ln_gain,
        ln_shift,
        qkv_full,
        bias_qv_full,
        proj_full,
        fc1_full,
        bias_fc1_full,
        fc2_full,
        bias_out,
        flats,
    )
    layer_out, grad_in = (
        lax.all_to_all(out_rows, "col", split_axis=1, concat_axis=0, tiled=True),
        lax.all_to_all(grad_rows, "col", split_axis=1, concat_axis=0, tiled=True),
    )
    summed = lax.psum(
        (grads[0], grads[1], grads[2], grads[3], grads[4], grads[5], grads[6], grads[7]),
        ("row", "col"),
    )
    return (
        layer_out,
        grad_in,
        summed[0].reshape(NA, R, D),
        summed[1].reshape(NA, R, 3, D),
        summed[2].reshape(NA, R, D),
        summed[3].reshape(NA, R, D),
        summed[4].reshape(NA, R, D),
        summed[5].reshape(NA, R, FF),
        summed[6].reshape(NA, R, FF),
        summed[7].reshape(NA, R, D),
    )


def solution(mesh):
    return jax.shard_map(
        per_device,
        mesh=mesh,
        in_specs=(
            P("row", "col"),
            P("row", "col"),
            P("row", None),
            P("row"),
            P(),
            P(),
            P(None, "row", "col"),
            P(None, "col"),
            P("col", "row"),
            P("row", "col"),
            P("col"),
            P("col", "row"),
            P(),
            P(),
            P(),
            P(),
            P(),
            P(),
            P(),
            P(),
            P(),
        ),
        out_specs=(P("row", "col"), P("row", "col"), P(), P(), P(), P(), P(), P(), P(), P()),
        check_vma=False,
    )
```

profile of v0, /device:TPU:0, one launch (start us, length us, event | category | flops | bytes accessed | tf_op | source)
XLA Modules:
  0.0 621.6 jit_solution(14303194922403295950)
XLA Ops:
  9.5 47.7 %all-gather.8.cloned.1.call-done = bf16[3,1024,256]{2,1,0:T(8,128)(2,1)} async-done(((bf16[3,128,256]{2,1,0:T(8,128)(2,1)}), bf16[3,1024,256]{2,1,0:T(8,128)(2,1)}) %all-gather.8.cloned.1.call-update) | async-done | bytes 1572880 | tf_op jit(solution)/shard_map/all_gather | solution.py:243
  57.3 30.8 %all_gather.33 = bf16[256,1024]{1,0:T(8,128)(2,1)} all-gather(bf16[256,128]{1,0:T(8,128)(2,1)} %param.29), channel_id=1, replica_groups=mesh['row'=8,'col'=4] {'row'}, dimensions={1}, use_global_device_ids=true | all-gather | bytes 589824 | tf_op jit(solution)/shard_map/all_gather | solution.py:244
  88.1 21.9 %all-gather.14.cloned.1.call-done = bf16[1024,1024]{1,0:T(8,128)(2,1)} async-done(((bf16[128,1024]{1,0:T(8,128)(2,1)}), bf16[1024,1024]{1,0:T(8,128)(2,1)}) %all-gather.14.cloned.1.call-update) | async-done | bytes 2097168 | tf_op jit(solution)/shard_map/all_gather | solution.py:245
  110.0 3.5 all-to-all-start
  113.6 11.0 %all_gather.32 = bf16[2,1024]{1,0:T(2,128)(2,1)S(1)} all-gather(bf16[2,256]{1,0:T(2,128)(2,1)S(1)} %copy-done.61), channel_id=1, replica_groups=mesh['row'=8,'col'=4] {'col'}, dimensions={1}, use_global_device_ids=true | all-gather | bytes 5120 | tf_op jit(solution)/shard_map/all_gather | solution.py:253
  124.9 5.2 all_gather.37
  131.6 29.4 %all-gather.18.cloned.1.call-done = bf16[1024,1024]{1,0:T(8,128)(2,1)} async-done(((bf16[1024,128]{1,0:T(8,128)(2,1)}), bf16[1024,1024]{1,0:T(8,128)(2,1)}) %all-gather.18.cloned.1.call-update) | async-done | bytes 2097168 | tf_op jit(solution)/shard_map/all_gather | solution.py:246
  161.6 3.5 all-to-all-start.2
  167.2 12.3 %all-to-all-done.2 = bf16[4,320,256]{2,1,0:T(8,128)(2,1)S(1)} async-done(((bf16[4,320,256]{2,1,0:T(8,128)(2,1)}), bf16[4,320,256]{2,1,0:T(8,128)(2,1)S(1)}, u32[]{:S(2)}, u32[]{:S(2)}) %all-to-all-start.2) | async-done | bytes 655392 | tf_op jit(solution)/shard_map/all_to_all | solution.py:258
  182.9 28.6 %all-gather.10.cloned.1.call-done = bf16[3,1024,1024]{2,1,0:T(8,128)(2,1)} async-done(((bf16[3,1024,256]{2,1,0:T(8,128)(2,1)}), bf16[3,1024,1024]{2,1,0:T(8,128)(2,1)}) %all-gather.10.cloned.1.call-update) | async-done | bytes 6291472 | tf_op jit(solution)/shard_map/all_gather | solution.py:249
  211.5 5.0 fusion.50
  216.5 1.7 add_bitcast_fusion
  218.3 1.9 copy-done.7
  220.6 3.3 fusion.63
  225.5 1.8 copy.87
  227.4 2.1 fusion.67
  230.7 2.0 copy-done.1
  232.7 2.0 fusion.32
  235.1 2.4 fusion.69
  237.6 2.3 fusion.68
  241.7 50.8 %all-gather.16.cloned.1.call-done = bf16[1024,4096]{1,0:T(8,128)(2,1)} async-done(((bf16[1024,1024]{1,0:T(8,128)(2,1)}), bf16[1024,4096]{1,0:T(8,128)(2,1)}) %all-gather.16.cloned.1.call-update) | async-done | bytes 8388624 | tf_op jit(solution)/shard_map/all_gather | solution.py:251
  292.5 5.4 fusion.70
  298.0 15.6 %fusion.7 = (bf16[320,4096]{1,0:T(8,128)(2,1)}, f32[320,4096]{1,0:T(8,128)}) fusion(f32[4096]{0:T(1024)S(1)} %convert_element_type.177, f32[320,4096]{1,0:T(8,128)S(1)} %fusion.70, f32[320,128]{1,0:T(8,128)S(1)} %convolution_multiply_fusion.2, bf16[128,4096]{1,0:T(8,128)(2,1)S(1)} %bitcast.152), kind=kOutput, calls=%fused_computation.17 | convolution fusion | flops 2101084160 | bytes 14336000 | tf_op jit(solution)/shard_map/tr,rf->tf/dot_general | solution.py:42
  313.6 38.8 %all-gather.20.cloned.1.call-done = bf16[4096,1024]{1,0:T(8,128)(2,1)} async-done(((bf16[1024,1024]{1,0:T(8,128)(2,1)}), bf16[4096,1024]{1,0:T(8,128)(2,1)}) %all-gather.20.cloned.1.call-update) | async-done | bytes 8388624 | tf_op jit(solution)/shard_map/all_gather | solution.py:252
  352.4 5.9 fusion.47
  358.3 4.8 fusion.4
  364.0 3.2 fusion.76
  368.0 3.2 fusion.77
  372.6 2.9 fusion.72
  379.5 1.8 fusion.74
  382.3 2.0 fusion.37
  385.7 5.6 fusion.33
  391.3 6.2 %multiply_reduce_fusion = (f32[16,320]{1,0:T(8,128)S(1)}, f32[16,320,320]{1,2,0:T(8,128)}) fusion(f32[16,320,320]{1,2,0:T(8,128)} %copy-done.1, f32[16,320]{1,0:T(8,128)S(1)} %log_add_fusion, bf16[320,16,64]{0,2,1:T(8,128)(2,1)S(1)} %bitcast.166, f32[320,16,64]{0,2,1:T(8,128)S(1)} %bitcast.173, f32[16,64]{1,0:T(8,128)S(1)} %add.191), kind=kOutput, calls=%fused_computation.1 | convolution fusion | flops 215280640 | bytes 15118336 | tf_op jit(solution)/shard_map/gqhd,gkhd->ghqk/dot_general | solution.py:38
  397.6 7.1 %multiply_convert_fusion = bf16[16,320,320]{1,2,0:T(8,128)(2,1)S(1)} fusion(f32[16,320,320]{1,2,0:T(8,128)} %get-tuple-element.42, f32[16,320,320]{1,2,0:T(8,128)} %copy-done.1, f32[16,320]{1,0:T(8,128)S(1)} %get-tuple-element.41, f32[16,320]{1,0:T(8,128)S(1)} %log_add_fusion), kind=kLoop, calls=%fused_computation | loop fusion | flops 6553600 | bytes 16424960 | tf_op jit(solution)/shard_map/convert_element_type | solution.py:67
  404.7 3.7 multiply_convert_fusion.1
  408.4 1.7 multiply_convert_fusion.2
  410.1 2.3 copy.99
  412.4 2.3 copy.97
  414.7 2.2 copy.98
  416.9 2.3 fusion.45
  420.8 2.0 fusion.43
  425.4 6.3 %fusion.71 = f32[320,1024]{1,0:T(8,128)S(1)} fusion(bf16[320,4096]{1,0:T(8,128)(2,1)} %get-tuple-element.38, bf16[4096,1024]{1,0:T(8,128)(2,1)} %all-gather.20.cloned.1.call-done), kind=kOutput, calls=%fused_computation.145 | convolution fusion | flops 2684354560 | bytes 12320768 | tf_op jit(solution)/shard_map/tf,fd->td/dot_general | solution.py:38
  433.5 3.5 all-to-all-start.1
  437.1 5.5 convolution_bitcast_fusion
  445.3 8.1 %all-to-all-done.1 = bf16[320,4,256]{2,0,1:T(8,128)(2,1)S(1)} async-done(((bf16[320,4,256]{2,0,1:T(8,128)(2,1)}), bf16[320,4,256]{2,0,1:T(8,128)(2,1)S(1)}, u32[]{:S(2)}, u32[]{:S(2)}) %all-to-all-start.1) | async-done | bytes 655392 | tf_op jit(solution)/shard_map/all_to_all | solution.py:281
  453.4 3.5 all-to-all-start.3
  456.9 10.2 %all-to-all-done.3 = bf16[320,4,256]{2,0,1:T(8,128)(2,1)S(1)} async-done(((bf16[320,4,256]{2,0,1:T(8,128)(2,1)}), bf16[320,4,256]{2,0,1:T(8,128)(2,1)S(1)}, u32[]{:S(2)}, u32[]{:S(2)}) %all-to-all-start.3) | async-done | bytes 655392 | tf_op jit(solution)/shard_map/all_to_all | solution.py:282
  467.1 138.0 %all-reduce.4.cloned.1.call-done = (f32[8,16,1024]{2,1,0:T(8,128)}, f32[8,16,3,1024]{3,1,2,0:T(8,128)}, f32[8,16,1024]{2,1,0:T(8,128)}, f32[8,16,1024]{2,1,0:T(8...) async-done(((f32[8,16,1024]{2,1,0:T(8,128)}, f32[8,16,3,1024]{3,1,2,0:T(8,128)}, ...) | async-done | bytes 8388624 | tf_op jit(solution)/shard_map/psum | solution.py:284
  (226 shorter events, 43.2 us)
Async XLA Ops:
  7.2 290.8 %copy-start = (bf16[8,16,4096]{2,1,0:T(8,128)(2,1)S(1)}, bf16[8,16,4096]{2,1,0:T(8,128)(2,1)}, u32[]{:S(2)}) copy-start(bf16[8,16,4096]{2,1,0:T(8,128)(2,1)} %param.39) | copy-start | bytes 3145732
  7.2 49.9 %all-gather.8.cloned.1.call-start = ((), (), s32[]{:S(2)}) async-start(), calls=%async_computation.4 | async-start | bytes 1769472 | tf_op jit(solution)/shard_map/all_gather | solution.py:243
  7.9 102.1 %all-gather.14.cloned.1.call-start = ((), (), s32[]{:S(2)}) async-start(), calls=%async_computation.7 | async-start | bytes 2359296 | tf_op jit(solution)/shard_map/all_gather | solution.py:245
  8.7 152.3 %all-gather.18.cloned.1.call-start = ((), (), s32[]{:S(2)}) async-start(), calls=%async_computation.9 | async-start | bytes 2359296 | tf_op jit(solution)/shard_map/all_gather | solution.py:246
  9.4 202.1 %all-gather.10.cloned.1.call-start = ((), (), s32[]{:S(2)}) async-start(), calls=%async_computation.5 | async-start | bytes 7864320 | tf_op jit(solution)/shard_map/all_gather | solution.py:249
  57.2 56.4 %copy-start.61 = (bf16[2,256]{1,0:T(2,128)(2,1)S(1)}, bf16[2,256]{1,0:T(2,128)(2,1)}, u32[]{:S(2)}) copy-start(bf16[2,256]{1,0:T(2,128)(2,1)} %param.28) | copy-start | bytes 3076
  57.2 67.5 %copy-start.62 = (s32[4]{0:T(128)S(1)}, s32[4]{0:T(128)}, u32[]{:S(2)}) copy-start(s32[4]{0:T(128)} %param.24) | copy-start | bytes 52
  57.2 67.6 %copy-start.55 = (s32[4,256]{1,0:T(4,128)S(1)}, s32[4,256]{1,0:T(4,128)}, u32[]{:S(2)}) copy-start(s32[4,256]{1,0:T(4,128)} %param.23) | copy-start | bytes 12292
  57.2 67.8 %copy-start.60 = (bf16[1024]{0:T(1024)(128)(2,1)S(1)}, bf16[1024]{0:T(1024)(128)(2,1)}, u32[]{:S(2)}) copy-start(bf16[1024]{0:T(1024)(128)(2,1)} %param.31) | copy-start | bytes 6148
  57.2 72.9 %copy-start.59 = (f32[2,1024]{1,0:T(2,128)S(1)}, f32[2,1024]{1,0:T(2,128)}, u32[]{:S(2)}) copy-start(f32[2,1024]{1,0:T(2,128)} %param.25) | copy-start | bytes 24580
  57.2 73.1 %copy-start.58 = (f32[2,1024]{1,0:T(2,128)S(1)}, f32[2,1024]{1,0:T(2,128)}, u32[]{:S(2)}) copy-start(f32[2,1024]{1,0:T(2,128)} %param.26) | copy-start | bytes 24580
  57.2 73.1 %copy-start.35 = (bf16[8,16,3,1024]{3,1,2,0:T(8,128)(2,1)S(1)}, bf16[8,16,3,1024]{3,1,2,0:T(8,128)(2,1)}, u32[]{:S(2)}) copy-start(bf16[8,16,3,1024]{3,1,2,0:T(8,128)(2,1)} %param.35) | copy-start | bytes 2359300
  57.2 177.9 %all-gather.12.cloned.1.call-start = ((), (), s32[]{:S(2)}) async-start(), calls=%async_computation.6 | async-start | bytes 2621440 | tf_op jit(solution)/shard_map/all_gather | solution.py:250
  88.1 204.4 %all-gather.16.cloned.1.call-start = ((), (), s32[]{:S(2)}) async-start(), calls=%async_computation.8 | async-start | bytes 10485760 | tf_op jit(solution)/shard_map/all_gather | solution.py:251
  110.0 51.0 %copy-start.56 = (bf16[2,1024]{1,0:T(2,128)(2,1)S(1)}, bf16[2,1024]{1,0:T(2,128)(2,1)}, u32[]{:S(2)}) copy-start(bf16[2,1024]{1,0:T(2,128)(2,1)} %param.33) | copy-start | bytes 12292
  110.0 51.6 %all-to-all-start = ((bf16[4,320,256]{2,1,0:T(8,128)(2,1)}), bf16[4,320,256]{2,1,0:T(8,128)(2,1)S(1)}, u32[]{:S(2)}, u32[]{:S(2)}) async-start(bf16[4,320,256]{2,1,0:T(8,128)(2,1)} %bitcast), calls=%async_computation | async-start | bytes 1310720 | tf_op jit(solution)/shard_map/all_to_all | solution.py:257
  113.5 238.8 %all-gather.20.cloned.1.call-start = ((), (), s32[]{:S(2)}) async-start(), calls=%async_computation.10 | async-start | bytes 10485760 | tf_op jit(solution)/shard_map/all_gather | solution.py:252
  130.2 52.5 %copy-start.53 = (f32[1,1024]{1,0:T(1,128)}, f32[1,1024]{1,0:T(1,128)S(1)}, u32[]{:S(2)}) copy-start(f32[1,1024]{1,0:T(1,128)S(1)} %get-tuple-element.44) | copy-start | bytes 12292
  161.6 17.9 %all-to-all-start.2 = ((bf16[4,320,256]{2,1,0:T(8,128)(2,1)}), bf16[4,320,256]{2,1,0:T(8,128)(2,1)S(1)}, u32[]{:S(2)}, u32[]{:S(2)}) async-start(bf16[4,320,256]{2,1,0:T(8,128)(2,1)} %bitcast.201), calls=%async_computation.2 | async-start | bytes 1310720 | tf_op jit(solution)/shard_map/all_to_all | solution.py:258
  165.1 440.0 %all-reduce.4.cloned.1.call-start = ((), (), s32[]{:S(2)}) async-start(), calls=%async_computation.11 | async-start | bytes 16777216 | tf_op jit(solution)/shard_map/psum | solution.py:284
  165.3 17.3 %copy-start.49 = (f32[320]{0:T(512)}, f32[320]{0:T(512)S(1)}, u32[]{:S(2)}) copy-start(f32[320]{0:T(512)S(1)} %broadcast_multiply_fusion.5) | copy-start | bytes 3844
  165.7 17.0 %copy-start.51 = (f32[320]{0:T(512)}, f32[320]{0:T(512)S(1)}, u32[]{:S(2)}) copy-start(f32[320]{0:T(512)S(1)} %add_rsqrt_fusion.1) | copy-start | bytes 3844
  167.2 15.4 %copy-start.2 = (f32[4,40,8,256]{3,2,0,1:T(8,128)}, f32[4,40,8,256]{3,2,0,1:T(8,128)S(1)}, u32[]{:S(2)}) copy-start(f32[4,40,8,256]{3,2,0,1:T(8,128)S(1)} %copy.108) | copy-start | bytes 3932164
  181.6 34.9 %copy-start.42 = (f32[320,128,1]{1,0,2:T(8,128)}, f32[320,128,1]{1,0,2:T(8,128)S(1)}, u32[]{:S(2)}) copy-start(f32[320,128,1]{1,0,2:T(8,128)S(1)} %fusion.46) | copy-start | bytes 491524
  182.9 33.6 %copy-start.21 = (bf16[320,1024]{1,0:T(8,128)(2,1)}, bf16[320,1024]{1,0:T(8,128)(2,1)S(1)}, u32[]{:S(2)}) copy-start(bf16[320,1024]{1,0:T(8,128)(2,1)S(1)} %add_convert_fusion.4) | copy-start | bytes 1966084
  182.9 33.6 %copy-start.17 = (bf16[8,16,3,1024]{3,1,0,2:T(8,128)(2,1)S(1)}, bf16[8,16,3,1024]{3,1,0,2:T(8,128)(2,1)}, u32[]{:S(2)}) copy-start(bf16[8,16,3,1024]{3,1,0,2:T(8,128)(2,1)} %copy.85) | copy-start | bytes 2359300
  220.6 6.7 %copy-start.11 = (bf16[1,320,1024]{1,2,0:T(8,128)(2,1)}, bf16[1,320,1024]{1,2,0:T(8,128)(2,1)S(1)}, u32[]{:S(2)}) copy-start(bf16[1,320,1024]{1,2,0:T(8,128)(2,1)S(1)} %copy.88) | copy-start | bytes 1966084
  352.4 5.9 copy-start.36
  352.4 5.9 copy-start.63
  352.4 5.9 copy-start.64
  363.1 9.5 %slice-start = ((s8[8388608]{0:T(1024)(128)(4,1)}), s8[4194304]{0:T(1024)(128)(4,1)S(1)}, s32[]{:S(2)}) async-start(s8[8388608]{0:T(1024)(128)(4,1)} %bitcast.210), calls=%async_computation.12 | async-start | bytes 8388608
  367.2 5.4 slice-start.1
  377.8 4.4 copy-start.4
  385.7 5.6 copy-start.14
  404.7 3.7 copy-start.12
  410.1 6.8 %copy-start.18 = (bf16[8,16,3,1024]{3,1,0,2:T(8,128)(2,1)S(1)}, bf16[8,16,3,1024]{3,1,0,2:T(8,128)(2,1)}, u32[]{:S(2)}) copy-start(bf16[8,16,3,1024]{3,1,0,2:T(8,128)(2,1)} %copy.85) | copy-start | bytes 2359300
  425.4 6.3 %copy-start.32 = (bf16[8,16,1024]{2,1,0:T(8,128)(2,1)S(1)}, bf16[8,16,1024]{2,1,0:T(8,128)(2,1)}, u32[]{:S(2)}) copy-start(bf16[8,16,1024]{2,1,0:T(8,128)(2,1)} %param.41) | copy-start | bytes 786436
  425.4 6.3 %copy-start.57 = (f32[1,1024]{1,0:T(1,128)S(1)}, f32[1,1024]{1,0:T(1,128)}, u32[]{:S(2)}) copy-start(f32[1,1024]{1,0:T(1,128)} %get-tuple-element.32) | copy-start | bytes 12292
  431.8 5.2 copy-start.38
  432.6 4.4 copy-start.40
  433.5 19.9 %all-to-all-start.1 = ((bf16[320,4,256]{2,0,1:T(8,128)(2,1)}), bf16[320,4,256]{2,0,1:T(8,128)(2,1)S(1)}, u32[]{:S(2)}, u32[]{:S(2)}) async-start(bf16[320,4,256]{2,0,1:T(8,128)(2,1)} %bitcast.151), calls=%async_computation.1 | async-start | bytes 1310720 | tf_op jit(solution)/shard_map/all_to_all | solution.py:281
  437.0 5.6 copy-start.3
  437.0 5.6 copy-start.34
  437.0 5.6 copy-start.50
  437.1 5.6 copy-start.52
  437.1 5.6 copy-start.54
  453.4 13.7 %all-to-all-start.3 = ((bf16[320,4,256]{2,0,1:T(8,128)(2,1)}), bf16[320,4,256]{2,0,1:T(8,128)(2,1)S(1)}, u32[]{:S(2)}, u32[]{:S(2)}) async-start(bf16[320,4,256]{2,0,1:T(8,128)(2,1)} %bitcast.150), calls=%async_computation.3 | async-start | bytes 1310720 | tf_op jit(solution)/shard_map/all_to_all | solution.py:282
  607.5 3.5 copy-start.24
  (31 other events, 66.9 us)
Sparse Core Ops, SparseCore 0:
  10.2 46.9 all-gather.7
  59.3 50.6 all-gather.13
  112.1 48.8 all-gather.17
  162.4 49.1 all-gather.9
  212.9 19.8 all-gather.11
  234.2 58.2 all-gather.15
  294.1 58.2 all-gather.19
  425.5 179.4 all-reduce.3
where the time goes:
time: 631 us; the launch traced here: 622 us
  waiting for transfers between devices  388 us (61%)
  matrix products  107 us (17%)
  blocking collectives  47 us (7%)
  local copies, waits for them, and re-layouts  38.4 us (6%)
  between operations  15.4 us (2%)
  starting transfers between devices  14.3 us (2%)
  other arithmetic  11.5 us (2%)
    psum x1, waiting for transfers between devices, per_device(): lax.psum((grads[0], grads[1], grads[2], grads[3], grads[4], grads[5], gra...  138 us
    dot_general x22, matrix products, narrow_dot(): jnp.einsum(formula, left_side, right_side, preferred_element_type=jnp.flo...  62.1 us
    all_gather x1, waiting for transfers between devices, per_device(): lax.all_gather(fc1_cols, 'col', axis=1, tiled=True)  50.8 us
    all_gather x1, waiting for transfers between devices, per_device(): lax.all_gather(w_qkv, 'row', axis=1, tiled=True)  47.7 us
    dot_general x16, matrix products, exact_dot(): jnp.einsum(formula, left_side, right_side, precision=highest, preferred_e...  45.2 us
    all_gather x1, waiting for transfers between devices, per_device(): lax.all_gather(fc2_rows, 'col', axis=0, tiled=True)  38.8 us
    all_gather x1, blocking collectives, per_device(): lax.all_gather(w_proj, 'row', axis=1, tiled=True)  30.8 us
    all_gather x1, waiting for transfers between devices, per_device(): lax.all_gather(w_fc2, 'row', axis=1, tiled=True)  29.4 us
  transfers between devices with their start and end apart: 12, of which 10 were waited for; matrix products, arithmetic and copies ran while one was open for 11% of the time, Pallas kernels for 0%

commit v1 on v0

--- a/solution.py
+++ b/solution.py
@@ -239,11 +239,33 @@
         fc2_down.reshape(rank_total, FF),
         fc2_up.reshape(rank_total, D),
     )
+
+    def _expand_samples_all(obj):
+        clean, current_arr, e_next = (lax.axis_size("row"), lax.axis_index("row"), obj.shape[1])
+        all_rows = [to_i * clean if ii == 1 else to_i for ii, to_i in enumerate(obj.shape)]
+        carry_in = lax.dynamic_update_slice_in_dim(
+            jnp.zeros(all_rows, obj.dtype), obj, current_arr * e_next, axis=1
+        )
+        x_new = x_now = obj
+        for w in [*range(1, clean // 2 + 1)]:
+            x_new = lax.ppermute(x_new, "row", [(ii, (ii + 1) % clean) for ii in range(clean)])
+            carry_in = lax.dynamic_update_slice_in_dim(
+                carry_in, x_new, (current_arr - w) % clean * e_next, axis=1
+            )
+            if 2 * w < clean:
+                x_now = lax.ppermute(
+                    x_now, "row", perm=[(ii, (ii - 1) % clean) for ii in range(clean)]
+                )
+                carry_in = lax.dynamic_update_slice_in_dim(
+                    carry_in, x_now, (current_arr + w) % clean * e_next, axis=1
+                )
+        return carry_in
+
     qkv_cols, proj_rows, fc1_cols, fc2_rows = (
         lax.all_gather(w_qkv, "row", axis=1, tiled=True),
         lax.all_gather(w_proj, "row", axis=1, tiled=True),
         lax.all_gather(w_fc1, "row", axis=0, tiled=True),
-        lax.all_gather(w_fc2, "row", axis=1, tiled=True),
+        _expand_samples_all(w_fc2),
     )
     qkv_full, proj_full, fc1_full, fc2_full, bias_qv_full, bias_fc1_full = (
         lax.all_gather(qkv_cols, "col", axis=2, tiled=True),

time: 631 us -> 583 us (0.924)
  waiting for transfers between devices: 388 us -> 287 us
  local copies, waits for them, and re-layouts: 38.4 us -> 65.3 us
  starting transfers between devices: 14.3 us -> 29.6 us
    all_gather x1, waiting for transfers between devices: 50.8 us -> 14 us  [per_device(): lax.all_gather(fc1_cols, 'col', axis=1, tiled=True)]
    all_gather x1 -> x0, waiting for transfers between devices: 29.4 us -> none  [per_device(): lax.all_gather(w_fc2, 'row', axis=1, tiled=True)]
    all_gather x1, waiting for transfers between devices: 28.6 us -> 0.01 us  [per_device(): lax.all_gather(qkv_cols, 'col', axis=2, tiled=True)]
    ppermute x0 -> x7, starting transfers between devices: none -> 14.6 us  [the longest x3 13 us: _expand_samples_all(): lax.ppermute(x_now, 'row', perm=[(ii, (ii - 1) % clean) for ii in range(c...]
    all_to_all x1, waiting for transfers between devices: 12.3 us -> 0.01 us  [per_device(): lax.all_to_all(grad_out, 'col', split_axis=0, concat_axis=1, tiled=True)]
    ppermute x0 -> x7, waiting for transfers between devices: none -> 8.84 us  [the longest x4 4.91 us: _expand_samples_all(): lax.ppermute(x_new, 'row', [(ii, (ii + 1) % clean) for ii in range(clean)])]
    dot_general x22, matrix products: 62.1 us -> 70 us  [narrow_dot(): jnp.einsum(formula, left_side, right_side, preferred_element_type=jnp.flo...]
    unnamed x145 -> x177, local copies, waits for them, and re-layouts: 16.4 us -> 20.4 us
  transfers between devices with their start and end apart: 12 -> 18, of which waited for: 10 -> 10; matrix products, arithmetic and copies ran while one was open for 11% -> 18% of each run, Pallas kernels for 0% -> 0%
where the time goes in v1:
time: 583 us; the launch traced here: 579 us
  waiting for transfers between devices  287 us (49%)
  matrix products  113 us (19%)
  local copies, waits for them, and re-layouts  65.3 us (11%)
  blocking collectives  52.9 us (9%)
  starting transfers between devices  29.6 us (5%)
  other arithmetic  15.4 us (3%)
  between operations  15.3 us (3%)
    psum x1, waiting for transfers between devices, per_device(): lax.psum((grads[0], grads[1], grads[2], grads[3], grads[4], grads[5], gra...  138 us
    dot_general x22, matrix products, narrow_dot(): jnp.einsum(formula, left_side, right_side, preferred_element_type=jnp.flo...  70 us
    all_gather x1, waiting for transfers between devices, per_device(): lax.all_gather(w_qkv, 'row', axis=1, tiled=True)  48.4 us
    dot_general x16, matrix products, exact_dot(): jnp.einsum(formula, left_side, right_side, precision=highest, preferred_e...  43.4 us
    all_gather x1, waiting for transfers between devices, per_device(): lax.all_gather(fc2_rows, 'col', axis=0, tiled=True)  39.1 us
    all_gather x1, blocking collectives, per_device(): lax.all_gather(w_proj, 'row', axis=1, tiled=True)  31 us
    all_gather x1, waiting for transfers between devices, per_device(): lax.all_gather(w_fc1, 'row', axis=0, tiled=True)  21.5 us
    unnamed x177, local copies, waits for them, and re-layouts  20.4 us
  transfers between devices with their start and end apart: 18, of which 10 were waited for; matrix products, arithmetic and copies ran while one was open for 18% of the time, Pallas kernels for 0%

profile of v1, /device:TPU:0, one launch (start us, length us, event | category | flops | bytes accessed | tf_op | source)
XLA Modules:
  0.0 579.3 jit_solution(6423102766796706566)
XLA Ops:
  8.7 48.4 %all-gather.7.cloned.1.call-done = bf16[3,1024,256]{2,1,0:T(8,128)(2,1)} async-done(((bf16[3,128,256]{2,1,0:T(8,128)(2,1)}), bf16[3,1024,256]{2,1,0:T(8,128)(2,1)}) %all-gather.7.cloned.1.call-update) | async-done | bytes 1572880 | tf_op jit(solution)/shard_map/all_gather | solution.py:265
  57.2 31.0 %all_gather.30 = bf16[256,1024]{1,0:T(8,128)(2,1)} all-gather(bf16[256,128]{1,0:T(8,128)(2,1)} %param.29), channel_id=1, replica_groups=mesh['row'=8,'col'=4] {'row'}, dimensions={1}, use_global_device_ids=true | all-gather | bytes 589824 | tf_op jit(solution)/shard_map/all_gather | solution.py:266
  88.3 21.5 %all-gather.13.cloned.1.call-done = bf16[1024,1024]{1,0:T(8,128)(2,1)} async-done(((bf16[128,1024]{1,0:T(8,128)(2,1)}), bf16[1024,1024]{1,0:T(8,128)(2,1)}) %all-gather.13.cloned.1.call-update) | async-done | bytes 2097168 | tf_op jit(solution)/shard_map/all_gather | solution.py:267
  109.9 1.9 collective-permute-start.1
  111.9 3.6 all-to-all-start
  115.6 16.5 %all_gather.29 = bf16[2,1024]{1,0:T(2,128)(2,1)S(1)} all-gather(bf16[2,256]{1,0:T(2,128)(2,1)S(1)} %copy-done.81), channel_id=1, replica_groups=mesh['row'=8,'col'=4] {'col'}, dimensions={1}, use_global_device_ids=true | all-gather | bytes 5120 | tf_op jit(solution)/shard_map/all_gather | solution.py:275
  142.7 5.5 all_gather.34
  157.2 3.4 collective-permute-start.3
  162.1 3.5 all-to-all-start.2
  166.7 7.6 %collective-permute-start.5 = (bf16[1024,128]{1,0:T(8,128)(2,1)S(1)}, bf16[1024,128]{1,0:T(8,128)(2,1)S(1)}, u32[]{:S(2)}, u32[]{:S(2)}) collective-permute-start(bf16[1024,128]{1,0:T(8,128)(2,1)S(1)} %collective-permute-done.3), channel_id=1, source_target_pairs={{0,28},{4,0},{8,4},{12,8},{16,12},{20,16},{24,20},{28,24},{1,29},{... | collective-permute-start | bytes 786440 | tf_op jit(solution)/shard_map/ppermute | solution.py:256
  176.5 3.0 collective-permute-done.5
  180.3 4.9 collective-permute-done.6
  192.4 4.6 fusion.72
  197.0 6.2 %fusion.49 = f32[320,3,1024]{2,0,1:T(8,128)S(1)} fusion(bf16[3,1024,1024]{2,1,0:T(8,128)(2,1)} %all-gather.9.cloned.1.call-done, bf16[320,1024]{1,0:T(8,128)(2,1)} %add_convert_fusion.4), kind=kOutput, calls=%fused_computation.102 | convolution fusion | flops 2013265920 | bytes 10878976 | tf_op jit(solution)/shard_map/td,cde->cte/dot_general | solution.py:38
  205.0 1.9 copy-done.6
  209.3 3.8 fusion.63
  213.1 3.0 copy.86
  216.0 2.9 copy.87
  219.0 3.5 fusion.67
  223.9 1.9 copy-done.1
  225.8 1.8 fusion.29
  228.1 2.5 fusion.69
  234.7 14.0 %all-gather.15.cloned.1.call-done = bf16[1024,4096]{1,0:T(8,128)(2,1)} async-done(((bf16[1024,1024]{1,0:T(8,128)(2,1)}), bf16[1024,4096]{1,0:T(8,128)(2,1)}) %all-gather.15.cloned.1.call-update) | async-done | bytes 8388624 | tf_op jit(solution)/shard_map/all_gather | solution.py:273
  248.7 5.5 fusion.70
  254.2 15.6 %fusion.7 = (bf16[320,4096]{1,0:T(8,128)(2,1)}, f32[320,4096]{1,0:T(8,128)}) fusion(f32[4096]{0:T(1024)S(1)} %copy-done.71, f32[320,4096]{1,0:T(8,128)S(1)} %fusion.70, f32[320,128]{1,0:T(8,128)S(1)} %copy-done.37, bf16[128,4096]{1,0:T(8,128)(2,1)S(1)} %bitcast.152), kind=kOutput, calls=%fused_computation.17 | convolution fusion | flops 2101084160 | bytes 14336000 | tf_op jit(solution)/shard_map/tr,rf->tf/dot_general | solution.py:42
  269.9 39.1 %all-gather.17.cloned.1.call-done = bf16[4096,1024]{1,0:T(8,128)(2,1)} async-done(((bf16[1024,1024]{1,0:T(8,128)(2,1)}), bf16[4096,1024]{1,0:T(8,128)(2,1)}) %all-gather.17.cloned.1.call-update) | async-done | bytes 8388624 | tf_op jit(solution)/shard_map/all_gather | solution.py:274
  309.0 9.6 %fusion.4 = bf16[320,4096]{1,0:T(8,128)(2,1)S(1)} fusion(f32[320,4096]{1,0:T(8,128)} %fusion.72, bf16[4096,1024]{1,0:T(8,128)(2,1)} %all-gather.17.cloned.1.call-done, f32[320,4096]{1,0:T(8,128)} %get-tuple-element.39, f32[320,1024]{1,0:T(8,128)} %bitcast.160, f32[320]{0:T(512)S(1)} %copy-done.63), kind=kOutput, calls=%fused_computation.14 | convolution fusion | flops 2699427840 | bytes 22807808 | tf_op jit(solution)/shard_map/td,fd->tf/dot_general | solution.py:38
  319.6 3.2 fusion.77
  324.2 2.9 fusion.73
  332.9 3.2 fusion.78
  336.1 1.8 fusion.75
  338.8 2.0 fusion.37
  342.3 5.6 fusion.30
  347.8 6.3 %multiply_reduce_fusion = (f32[16,320]{1,0:T(8,128)S(1)}, f32[16,320,320]{1,2,0:T(8,128)}) fusion(f32[16,320,320]{1,2,0:T(8,128)} %copy-done.1, f32[16,320]{1,0:T(8,128)S(1)} %log_add_fusion, bf16[320,16,64]{0,2,1:T(8,128)(2,1)S(1)} %bitcast.166, f32[320,16,64]{0,2,1:T(8,128)S(1)} %bitcast.173, f32[16,64]{1,0:T(8,128)S(1)} %copy-done.65), kind=kOutput, calls=%fused_computation.1 | convolution fusion | flops 215280640 | bytes 15118336 | tf_op jit(solution)/shard_map/gqhd,gkhd->ghqk/dot_general | solution.py:38
  354.1 7.1 %multiply_convert_fusion = bf16[16,320,320]{1,2,0:T(8,128)(2,1)S(1)} fusion(f32[16,320,320]{1,2,0:T(8,128)} %get-tuple-element.42, f32[16,320,320]{1,2,0:T(8,128)} %copy-done.1, f32[16,320]{1,0:T(8,128)S(1)} %get-tuple-element.41, f32[16,320]{1,0:T(8,128)S(1)} %log_add_fusion), kind=kLoop, calls=%fused_computation | loop fusion | flops 6553600 | bytes 16424960 | tf_op jit(solution)/shard_map/convert_element_type | solution.py:67
  361.3 3.7 multiply_convert_fusion.1
  366.7 2.3 copy.99
  369.0 2.2 copy.97
  371.2 2.3 copy.98
  373.5 2.3 fusion.45
  377.4 2.0 fusion.43
  383.6 7.6 %fusion.36 = bf16[320,1024]{1,0:T(8,128)(2,1)S(1)} fusion(f32[320,1024]{1,0:T(8,128)} %copy-done.2, f32[320,1024]{1,0:T(8,128)S(1)} %fusion.71, bf16[320,4096]{1,0:T(8,128)(2,1)} %get-tuple-element.38, bf16[4096,1024]{1,0:T(8,128)(2,1)} %all-gather.17.cloned.1.call-done, f32[1024]{0:T(1024)S(1)} %bitcast.212, f32[320]{0:T(512)S(1)} %copy-done.63), kind=kOutput, calls=%fused_computation.68 | convolution fusion | flops 2685992960 | bytes 14292224 | tf_op jit(solution)/shard_map/tf,fd->td/dot_general | solution.py:38
  392.1 3.7 all-to-all-start.1
  395.8 5.8 %convolution_bitcast_fusion = f32[320,1024]{1,0:T(8,128)S(1)} fusion(bf16[3,1024,1024]{2,1,0:T(8,128)(2,1)} %all-gather.9.cloned.1.call-done, bf16[1,320,1024]{2,1,0:T(8,128)(2,1)} %copy.99, bf16[1,320,1024]{2,1,0:T(8,128)(2,1)} %copy.98, bf16[1,320,1024]{2,1,0:T(8,128)(2,1)} %copy.97), kind=kOutput, calls=%fused_computation.61 | convolution fusion | flops 2015232000 | bytes 9568256 | tf_op jit(solution)/shard_map/cte,cde->td/dot_general | solution.py:38
  404.3 5.7 all-to-all-done.1
  410.0 3.5 all-to-all-start.3
  413.4 10.2 %all-to-all-done.3 = bf16[320,4,256]{2,0,1:T(8,128)(2,1)S(1)} async-done(((bf16[320,4,256]{2,0,1:T(8,128)(2,1)}), bf16[320,4,256]{2,0,1:T(8,128)(2,1)S(1)}, u32[]{:S(2)}, u32[]{:S(2)}) %all-to-all-start.3) | async-done | bytes 655392 | tf_op jit(solution)/shard_map/all_to_all | solution.py:304
  423.6 138.1 %all-reduce.4.cloned.1.call-done = (f32[8,16,1024]{2,1,0:T(8,128)}, f32[8,16,3,1024]{3,1,2,0:T(8,128)}, f32[8,16,1024]{2,1,0:T(8,128)}, f32[8,16,1024]{2,1,0:T(8...) async-done(((f32[8,16,1024]{2,1,0:T(8,128)}, f32[8,16,3,1024]{3,1,2,0:T(8,128)}, ...) | async-done | bytes 8388624 | tf_op jit(solution)/shard_map/psum | solution.py:306
  (277 shorter events, 75.9 us)
Async XLA Ops:
  7.2 247.0 %copy-start = (bf16[8,16,4096]{2,1,0:T(8,128)(2,1)S(1)}, bf16[8,16,4096]{2,1,0:T(8,128)(2,1)}, u32[]{:S(2)}) copy-start(bf16[8,16,4096]{2,1,0:T(8,128)(2,1)} %param.39) | copy-start | bytes 3145732
  7.2 49.9 %all-gather.7.cloned.1.call-start = ((), (), s32[]{:S(2)}) async-start(), calls=%async_computation.4 | async-start | bytes 1769472 | tf_op jit(solution)/shard_map/all_gather | solution.py:265
  7.9 101.9 %all-gather.13.cloned.1.call-start = ((), (), s32[]{:S(2)}) async-start(), calls=%async_computation.7 | async-start | bytes 2359296 | tf_op jit(solution)/shard_map/all_gather | solution.py:267
  8.7 188.3 %all-gather.9.cloned.1.call-start = ((), (), s32[]{:S(2)}) async-start(), calls=%async_computation.5 | async-start | bytes 7864320 | tf_op jit(solution)/shard_map/all_gather | solution.py:271
  57.1 52.7 %copy-start.49 = (bf16[1024,128]{1,0:T(8,128)(2,1)S(1)}, bf16[1024,128]{1,0:T(8,128)(2,1)}, u32[]{:S(2)}) copy-start(bf16[1024,128]{1,0:T(8,128)(2,1)} %param.32) | copy-start | bytes 786436
  57.2 170.9 %all-gather.11.cloned.1.call-start = ((), (), s32[]{:S(2)}) async-start(), calls=%async_computation.6 | async-start | bytes 2621440 | tf_op jit(solution)/shard_map/all_gather | solution.py:272
  88.2 27.4 %copy-start.81 = (bf16[2,256]{1,0:T(2,128)(2,1)S(1)}, bf16[2,256]{1,0:T(2,128)(2,1)}, u32[]{:S(2)}) copy-start(bf16[2,256]{1,0:T(2,128)(2,1)} %param.28) | copy-start | bytes 3076
  88.2 43.8 %copy-start.77 = (f32[2,1024]{1,0:T(2,128)S(1)}, f32[2,1024]{1,0:T(2,128)}, u32[]{:S(2)}) copy-start(f32[2,1024]{1,0:T(2,128)} %param.26) | copy-start | bytes 24580
  88.2 45.0 %copy-start.78 = (f32[2,1024]{1,0:T(2,128)S(1)}, f32[2,1024]{1,0:T(2,128)}, u32[]{:S(2)}) copy-start(f32[2,1024]{1,0:T(2,128)} %param.25) | copy-start | bytes 24580
  88.2 46.2 %copy-start.73 = (bf16[2,1024]{1,0:T(2,128)(2,1)S(1)}, bf16[2,1024]{1,0:T(2,128)(2,1)}, u32[]{:S(2)}) copy-start(bf16[2,1024]{1,0:T(2,128)(2,1)} %param.33) | copy-start | bytes 12292
  88.2 46.8 %copy-start.72 = (s32[4,256]{1,0:T(4,128)S(1)}, s32[4,256]{1,0:T(4,128)}, u32[]{:S(2)}) copy-start(s32[4,256]{1,0:T(4,128)} %param.23) | copy-start | bytes 12292
  88.3 160.5 %all-gather.15.cloned.1.call-start = ((), (), s32[]{:S(2)}) async-start(), calls=%async_computation.8 | async-start | bytes 10485760 | tf_op jit(solution)/shard_map/all_gather | solution.py:273
  109.9 47.4 %collective-permute-start.1 = (bf16[1024,128]{1,0:T(8,128)(2,1)S(1)}, bf16[1024,128]{1,0:T(8,128)(2,1)S(1)}, u32[]{:S(2)}, u32[]{:S(2)}) collective-permute-start(bf16[1024,128]{1,0:T(8,128)(2,1)S(1)} %copy-done.49), channel_id=1, source_target_pairs={{0,28},{4,0},{8,4},{12,8},{16,12},{20,16},{24,20},{28,24},{1,29},{... | collective-permute-start | bytes 786440 | tf_op jit(solution)/shard_map/ppermute | solution.py:256
  111.8 26.3 %collective-permute-start = (bf16[1024,128]{1,0:T(8,128)(2,1)S(1)}, bf16[1024,128]{1,0:T(8,128)(2,1)S(1)}, u32[]{:S(2)}, u32[]{:S(2)}) collective-permute-start(bf16[1024,128]{1,0:T(8,128)(2,1)S(1)} %copy-done.49), channel_id=1, source_target_pairs={{0,4},{4,8},{8,12},{12,16},{16,20},{20,24},{24,28},{28,0},{1,5},{5... | collective-permute-start | bytes 786440 | tf_op jit(solution)/shard_map/ppermute | solution.py:251
  111.9 40.9 %copy-start.36 = (bf16[8,16,3,1024]{3,1,2,0:T(8,128)(2,1)S(1)}, bf16[8,16,3,1024]{3,1,2,0:T(8,128)(2,1)}, u32[]{:S(2)}) copy-start(bf16[8,16,3,1024]{3,1,2,0:T(8,128)(2,1)} %param.35) | copy-start | bytes 2359300
  111.9 50.1 %all-to-all-start = ((bf16[4,320,256]{2,1,0:T(8,128)(2,1)}), bf16[4,320,256]{2,1,0:T(8,128)(2,1)S(1)}, u32[]{:S(2)}, u32[]{:S(2)}) async-start(bf16[4,320,256]{2,1,0:T(8,128)(2,1)} %bitcast), calls=%async_computation | async-start | bytes 1310720 | tf_op jit(solution)/shard_map/all_to_all | solution.py:279
  134.4 56.8 %copy-start.56 = (f32[1,1024]{1,0:T(1,128)}, f32[1,1024]{1,0:T(1,128)S(1)}, u32[]{:S(2)}) copy-start(f32[1,1024]{1,0:T(1,128)S(1)} %get-tuple-element.44) | copy-start | bytes 12292
  138.0 24.1 %collective-permute-start.2 = (bf16[1024,128]{1,0:T(8,128)(2,1)S(1)}, bf16[1024,128]{1,0:T(8,128)(2,1)S(1)}, u32[]{:S(2)}, u32[]{:S(2)}) collective-permute-start(bf16[1024,128]{1,0:T(8,128)(2,1)S(1)} %collective-permute-done), channel_id=1, source_target_pairs={{0,4},{4,8},{8,12},{12,16},{16,20},{20,24},{24,28},{28,0},{1,5},{5... | collective-permute-start | bytes 786440 | tf_op jit(solution)/shard_map/ppermute | solution.py:251
  151.5 67.4 %copy-start.52 = (f32[16,64]{1,0:T(8,128)}, f32[16,64]{1,0:T(8,128)S(1)}, u32[]{:S(2)}) copy-start(f32[16,64]{1,0:T(8,128)S(1)} %add.254) | copy-start | bytes 12292
  157.2 9.5 %collective-permute-start.3 = (bf16[1024,128]{1,0:T(8,128)(2,1)S(1)}, bf16[1024,128]{1,0:T(8,128)(2,1)S(1)}, u32[]{:S(2)}, u32[]{:S(2)}) collective-permute-start(bf16[1024,128]{1,0:T(8,128)(2,1)S(1)} %collective-permute-done.1), channel_id=1, source_target_pairs={{0,28},{4,0},{8,4},{12,8},{16,12},{20,16},{24,20},{28,24},{1,29},{... | collective-permute-start | bytes 786440 | tf_op jit(solution)/shard_map/ppermute | solution.py:256
  162.1 13.0 %collective-permute-start.4 = (bf16[1024,128]{1,0:T(8,128)(2,1)S(1)}, bf16[1024,128]{1,0:T(8,128)(2,1)S(1)}, u32[]{:S(2)}, u32[]{:S(2)}) collective-permute-start(bf16[1024,128]{1,0:T(8,128)(2,1)S(1)} %collective-permute-done.2), channel_id=1, source_target_pairs={{0,4},{4,8},{8,12},{12,16},{16,20},{20,24},{24,28},{28,0},{1,5},{5... | collective-permute-start | bytes 786440 | tf_op jit(solution)/shard_map/ppermute | solution.py:251
  162.1 26.3 %all-to-all-start.2 = ((bf16[4,320,256]{2,1,0:T(8,128)(2,1)}), bf16[4,320,256]{2,1,0:T(8,128)(2,1)S(1)}, u32[]{:S(2)}, u32[]{:S(2)}) async-start(bf16[4,320,256]{2,1,0:T(8,128)(2,1)} %bitcast.203), calls=%async_computation.2 | async-start | bytes 1310720 | tf_op jit(solution)/shard_map/all_to_all | solution.py:280
  165.6 143.4 %all-gather.17.cloned.1.call-start = ((), (), s32[]{:S(2)}) async-start(), calls=%async_computation.9 | async-start | bytes 10485760 | tf_op jit(solution)/shard_map/all_gather | solution.py:274
  166.7 12.9 %collective-permute-start.5 = (bf16[1024,128]{1,0:T(8,128)(2,1)S(1)}, bf16[1024,128]{1,0:T(8,128)(2,1)S(1)}, u32[]{:S(2)}, u32[]{:S(2)}) collective-permute-start(bf16[1024,128]{1,0:T(8,128)(2,1)S(1)} %collective-permute-done.3), channel_id=1, source_target_pairs={{0,28},{4,0},{8,4},{12,8},{16,12},{20,16},{24,20},{28,24},{1,29},{... | collective-permute-start | bytes 786440 | tf_op jit(solution)/shard_map/ppermute | solution.py:256
  175.1 10.1 %collective-permute-start.6 = (bf16[1024,128]{1,0:T(8,128)(2,1)S(1)}, bf16[1024,128]{1,0:T(8,128)(2,1)S(1)}, u32[]{:S(2)}, u32[]{:S(2)}) collective-permute-start(bf16[1024,128]{1,0:T(8,128)(2,1)S(1)} %collective-permute-done.4), channel_id=1, source_target_pairs={{0,4},{4,8},{8,12},{12,16},{16,20},{20,24},{24,28},{28,0},{1,5},{5... | collective-permute-start | bytes 786440 | tf_op jit(solution)/shard_map/ppermute | solution.py:251
  175.8 11.1 %copy-start.68 = (f32[4,256]{1,0:T(4,128)S(1)}, f32[4,256]{1,0:T(4,128)}, u32[]{:S(2)}) copy-start(f32[4,256]{1,0:T(4,128)} %mul.257) | copy-start | bytes 12292
  175.8 11.1 %copy-start.69 = (f32[4,256]{1,0:T(4,128)S(1)}, f32[4,256]{1,0:T(4,128)}, u32[]{:S(2)}) copy-start(f32[4,256]{1,0:T(4,128)} %add.245) | copy-start | bytes 12292
  185.9 375.8 %all-reduce.4.cloned.1.call-start = ((), (), s32[]{:S(2)}) async-start(), calls=%async_computation.10 | async-start | bytes 16777216 | tf_op jit(solution)/shard_map/psum | solution.py:306
  190.9 12.3 %copy-start.42 = (f32[320,128,1]{1,0,2:T(8,128)}, f32[320,128,1]{1,0,2:T(8,128)S(1)}, u32[]{:S(2)}) copy-start(f32[320,128,1]{1,0,2:T(8,128)S(1)} %fusion.46) | copy-start | bytes 491524
  197.0 6.3 %copy-start.16 = (bf16[8,16,3,1024]{3,1,0,2:T(8,128)(2,1)S(1)}, bf16[8,16,3,1024]{3,1,0,2:T(8,128)(2,1)}, u32[]{:S(2)}) copy-start(bf16[8,16,3,1024]{3,1,0,2:T(8,128)(2,1)} %copy.85) | copy-start | bytes 2359300
  209.2 9.7 %copy-start.10 = (bf16[1,320,1024]{1,2,0:T(8,128)(2,1)}, bf16[1,320,1024]{1,2,0:T(8,128)(2,1)S(1)}, u32[]{:S(2)}) copy-start(bf16[1,320,1024]{1,2,0:T(8,128)(2,1)S(1)} %copy.88) | copy-start | bytes 1966084
  234.7 19.5 %copy-start.71 = (f32[4096]{0:T(1024)S(1)}, f32[4096]{0:T(1024)}, u32[]{:S(2)}) copy-start(f32[4096]{0:T(1024)} %convert_element_type.177) | copy-start | bytes 49156
  248.7 5.5 copy-start.37
  254.2 54.8 %copy-start.63 = (f32[320]{0:T(512)S(1)}, f32[320]{0:T(512)}, u32[]{:S(2)}) copy-start(f32[320]{0:T(512)} %fusion.54) | copy-start | bytes 3844
  309.0 9.6 %copy-start.76 = (s32[128]{0:T(128)S(1)}, s32[128]{0:T(128)}, u32[]{:S(2)}) copy-start(s32[128]{0:T(128)} %and_select_fusion) | copy-start | bytes 1540
  318.7 5.5 copy-start.82
  329.4 8.5 %copy-start.4 = (f32[320,1024]{1,0:T(8,128)}, f32[320,1024]{1,0:T(8,128)S(1)}, u32[]{:S(2)}) copy-start(f32[320,1024]{1,0:T(8,128)S(1)} %multiply_add_fusion) | copy-start | bytes 3932164
  332.9 4.9 copy-start.9
  342.2 5.6 copy-start.13
  342.2 5.6 copy-start.65
  354.1 7.1 %copy-start.53 = (f32[16,64]{1,0:T(8,128)S(1)}, f32[16,64]{1,0:T(8,128)}, u32[]{:S(2)}) copy-start(f32[16,64]{1,0:T(8,128)} %copy-done.52) | copy-start | bytes 12292
  366.7 6.8 %copy-start.17 = (bf16[8,16,3,1024]{3,1,0,2:T(8,128)(2,1)S(1)}, bf16[8,16,3,1024]{3,1,0,2:T(8,128)(2,1)}, u32[]{:S(2)}) copy-start(bf16[8,16,3,1024]{3,1,0,2:T(8,128)(2,1)} %copy.85) | copy-start | bytes 2359300
  392.1 17.9 %all-to-all-start.1 = ((bf16[320,4,256]{2,0,1:T(8,128)(2,1)}), bf16[320,4,256]{2,0,1:T(8,128)(2,1)S(1)}, u32[]{:S(2)}, u32[]{:S(2)}) async-start(bf16[320,4,256]{2,0,1:T(8,128)(2,1)} %bitcast.181), calls=%async_computation.1 | async-start | bytes 1310720 | tf_op jit(solution)/shard_map/all_to_all | solution.py:303
  395.7 5.9 %copy-start.33 = (bf16[8,16,1024]{2,1,0:T(8,128)(2,1)S(1)}, bf16[8,16,1024]{2,1,0:T(8,128)(2,1)}, u32[]{:S(2)}) copy-start(bf16[8,16,1024]{2,1,0:T(8,128)(2,1)} %param.34) | copy-start | bytes 786436
  395.7 5.9 %copy-start.51 = (f32[320]{0:T(512)S(1)}, f32[320]{0:T(512)}, u32[]{:S(2)}) copy-start(f32[320]{0:T(512)} %copy-done.50) | copy-start | bytes 3844
  395.8 5.9 %copy-start.55 = (f32[320]{0:T(512)S(1)}, f32[320]{0:T(512)}, u32[]{:S(2)}) copy-start(f32[320]{0:T(512)} %copy-done.54) | copy-start | bytes 3844
  395.8 5.9 %copy-start.57 = (f32[1,1024]{1,0:T(1,128)S(1)}, f32[1,1024]{1,0:T(1,128)}, u32[]{:S(2)}) copy-start(f32[1,1024]{1,0:T(1,128)} %copy-done.56) | copy-start | bytes 12292
  410.0 13.7 %all-to-all-start.3 = ((bf16[320,4,256]{2,0,1:T(8,128)(2,1)}), bf16[320,4,256]{2,0,1:T(8,128)(2,1)S(1)}, u32[]{:S(2)}, u32[]{:S(2)}) async-start(bf16[320,4,256]{2,0,1:T(8,128)(2,1)} %bitcast.150), calls=%async_computation.3 | async-start | bytes 1310720 | tf_op jit(solution)/shard_map/all_to_all | solution.py:304
  (53 other events, 114.0 us)
Sparse Core Ops, SparseCore 0:
  10.2 46.9 all-gather.6
  59.3 50.5 all-gather.12
  111.4 50.6 all-gather.8
  163.5 25.0 all-gather.10
  190.0 58.7 all-gather.14
  250.7 58.2 all-gather.16
  382.1 179.5 all-reduce.3
